TPU v7x, 32 devices: a whole 2x2x4 slice. The times are simulated.
32 devices in a mesh: outer: 4 (over y, x), inner: 8 (over z, core).
Axes of the slice: x: 2, y: 2, z: 4, core: 2. Of those that a mesh axis runs over, the one named last changes fastest.
Arguments:
- queries: bfloat16 [4096, 4096], P(('outer', 'inner')), may hold values from -24 to 24, as said below
- keys: bfloat16 [4096, 1024], P(('outer', 'inner')), may hold values from -24 to 24, as said below
- values: bfloat16 [4096, 1024], P(('outer', 'inner')), may hold values from -6 to 6
Outputs:
- attended: bfloat16 [4096, 4096], P(('outer', 'inner'))
Inputs may be any that keep to these rules, and one draw needn't show every extreme that they name: `queries`: entries of order one, a few larger. `keys`: entries of order one, a few larger.
All inputs are finite; a program needn't handle non-finite values.
Results may differ from a plain program's by a relative error of at most 0.008.
Values may be sent and summed in bfloat16 or wider, within the bound.
No kernel may reach another device: no remote copies, remote signals or barrier semaphores. Data moves between devices by JAX's collectives and lax.ppermute only.
A program may use at most 128 MiB of HBM per device.

v0:
```python
import jax
import jax.numpy as jnp
from jax import lax
from jax.sharding import PartitionSpec as P

QH = 32
KVH = 8
HD = 128


def shifted(block, axis, distance):
    devices = range(lax.axis_size(axis))
    route = [(i - distance, i) for i in devices if i - distance in devices]
    return lax.ppermute(block, axis, route)


def attend(state, near_keys, near_values, allowed, grouped):
    rows = near_keys.shape[0]
    heads = near_keys.shape[1]
    size = 256
    count = rows // size
    scale = 1.0 / HD**0.5
    key_blocks = near_keys.reshape(count, size, heads, HD)
    value_blocks = near_values.reshape(count, size, heads, HD)

    def one_block(carry, pieces):
        peak, total, accum = carry
        key_block, value_block = pieces
        scores = (
            jnp.einsum("qgrd,kgd->grqk", grouped, key_block, preferred_element_type=jnp.float32)
            * scale
        )
        scores = jnp.where(allowed, scores, -jnp.inf)
        upper = jnp.maximum(peak, jnp.max(scores, axis=-1))
        factor = jnp.exp(peak - upper)
        weights = jnp.exp(scores - upper[..., None])
        total = total * factor + jnp.sum(weights, axis=-1)
        update = jnp.einsum(
            "grqk,kgd->grqd",
            weights.astype(jnp.bfloat16),
            value_block,
            preferred_element_type=jnp.float32,
        )
        accum = accum * factor[..., None] + update
        return ((upper, total, accum), None)

    state, unused = lax.scan(one_block, state, (key_blocks, value_blocks))
    return state


def fresh_state(heads, ratio, tokens):
    return (
        jnp.full((heads, ratio, tokens), -jnp.inf, jnp.float32),
        jnp.zeros((heads, ratio, tokens), jnp.float32),
        jnp.zeros((heads, ratio, tokens, HD), jnp.float32),
    )


def shards(queries, keys, values):
    tokens = queries.shape[0]
    position = lax.axis_index("outer")
    before_ok = position > 0
    after_ok = position < lax.axis_size("outer") - 1
    members = lax.axis_size("inner")
    per_device = QH // members
    repeat = members // KVH
    query_heads = queries.reshape(tokens, QH, HD)
    key_heads = jnp.repeat(keys.reshape(tokens, KVH, HD), repeat, axis=1)
    value_heads = jnp.repeat(values.reshape(tokens, KVH, HD), repeat, axis=1)
    group_q, group_k, group_v = (
        lax.all_to_all(query_heads, "inner", split_axis=1, concat_axis=0, tiled=True),
        lax.all_to_all(key_heads, "inner", split_axis=1, concat_axis=0, tiled=True),
        lax.all_to_all(value_heads, "inner", split_axis=1, concat_axis=0, tiled=True),
    )
    rows = group_q.shape[0]
    grouped = group_q.reshape(rows, 1, per_device, HD)
    state = attend(fresh_state(1, per_device, rows), group_k, group_v, True, grouped)
    early_k, early_v = shifted((group_k, group_v), "outer", 1)
    state = attend(state, early_k, early_v, before_ok, grouped)
    late_k, late_v = shifted((group_k, group_v), "outer", -1)
    state = attend(state, late_k, late_v, after_ok, grouped)
    peak, total, accum = state
    mixed = (accum / total[..., None]).astype(jnp.bfloat16)
    mixed = mixed.reshape(per_device, rows, HD).transpose(1, 0, 2)
    back = lax.all_to_all(mixed, "inner", split_axis=0, concat_axis=1, tiled=True)
    return back.reshape(tokens, QH * HD)


def solution(mesh):
    placed = (P(("outer", "inner"), None), P(("outer", "inner"), None), P(("outer", "inner"), None))
    return jax.shard_map(
        shards, mesh=mesh, in_specs=placed, out_specs=P(("outer", "inner"), None), check_vma=False
    )
```

profile of v0, /device:TPU:0, one launch (start us, length us, event | category | flops | bytes accessed | tf_op | source)
XLA Modules:
  0.0 174.7 jit_solution(10812905736298252282)
XLA Ops:
  0.0 0.9 copy-done
  1.0 0.8 copy_bitcast_fusion.1
  1.7 6.4 %all-to-all-start = ((bf16[128,8,128]{2,0,1:T(8,128)(2,1)}), bf16[128,8,128]{2,0,1:T(8,128)(2,1)S(1)}, u32[]{:S(2)}, u32[]{:S(2)}) async-start(bf16[128,8,128]{2,0,1:T(8,128)(2,1)} %copy_bitcast_fusion.1), calls=%async_computation | async-start | bytes 524288 | tf_op jit(solution)/shard_map/all_to_all | solution.py:72
  8.1 1.7 copy_bitcast_fusion
  9.8 8.0 %all-to-all-done = bf16[128,8,128]{2,0,1:T(8,128)(2,1)S(1)} async-done(((bf16[128,8,128]{2,0,1:T(8,128)(2,1)}), bf16[128,8,128]{2,0,1:T(8,128)(2,1)S(1)}, u32[]{:S(2)}, u32[]{:S(2)}) %all-to-all-start) | async-done | bytes 262176 | tf_op jit(solution)/shard_map/all_to_all | solution.py:72
  17.8 3.4 %all-to-all-start.2 = ((bf16[128,8,128]{2,0,1:T(8,128)(2,1)}), bf16[128,8,128]{2,0,1:T(8,128)(2,1)S(1)}, u32[]{:S(2)}, u32[]{:S(2)}) async-start(bf16[128,8,128]{2,0,1:T(8,128)(2,1)} %copy_bitcast_fusion), calls=%async_computation.2 | async-start | bytes 524288 | tf_op jit(solution)/shard_map/all_to_all | solution.py:73
  21.2 2.3 %copy.29 = bf16[128,4096]{0,1:T(8,128)(2,1)} copy(bf16[128,4096]{1,0:T(8,128)(2,1)} %param.9) | data formatting | bytes 2097152 | tf_op args[0]
  23.5 7.4 %all-to-all-done.2 = bf16[128,8,128]{2,0,1:T(8,128)(2,1)S(1)} async-done(((bf16[128,8,128]{2,0,1:T(8,128)(2,1)}), bf16[128,8,128]{2,0,1:T(8,128)(2,1)S(1)}, u32[]{:S(2)}, u32[]{:S(2)}) %all-to-all-start.2) | async-done | bytes 262176 | tf_op jit(solution)/shard_map/all_to_all | solution.py:73
  30.8 0.7 copy-done.4
  31.5 3.6 %all-to-all-start.1 = ((bf16[128,32,128]{0,2,1:T(8,128)(2,1)}), bf16[128,32,128]{0,2,1:T(8,128)(2,1)S(1)}, u32[]{:S(2)}, u32[]{:S(2)}) async-start(bf16[128,32,128]{0,2,1:T(8,128)(2,1)} %bitcast.31), calls=%async_computation.1 | async-start | bytes 2097152 | tf_op jit(solution)/shard_map/all_to_all | solution.py:71
  35.1 4.1 %collective-permute-start = (bf16[1024,1,128]{2,0,1:T(8,128)(2,1)}, bf16[1024,1,128]{2,0,1:T(8,128)(2,1)}, u32[]{:S(2)}, u32[]{:S(2)}) collective-permute-start(bf16[1024,1,128]{2,0,1:T(8,128)(2,1)} %bitcast.261), channel_id=1, source_target_pairs={{0,8},{8,16},{16,24},{1,9},{9,17},{17,25},{2,10},{10,18},{18,26},{... | collective-permute-start | bytes 786440 | tf_op jit(solution)/shard_map/ppermute | solution.py:14
  39.3 1.3 collective-permute-start.2
  40.5 5.3 %collective-permute-start.1 = (bf16[1024,1,128]{2,0,1:T(8,128)(2,1)}, bf16[1024,1,128]{2,0,1:T(8,128)(2,1)}, u32[]{:S(2)}, u32[]{:S(2)}) collective-permute-start(bf16[1024,1,128]{2,0,1:T(8,128)(2,1)} %bitcast.264), channel_id=1, source_target_pairs={{0,8},{8,16},{16,24},{1,9},{9,17},{17,25},{2,10},{10,18},{18,26},{... | collective-permute-start | bytes 786440 | tf_op jit(solution)/shard_map/ppermute | solution.py:14
  45.8 1.3 collective-permute-start.3
  47.1 14.5 %all-to-all-done.1 = bf16[128,32,128]{0,2,1:T(8,128)(2,1)S(1)} async-done(((bf16[128,32,128]{0,2,1:T(8,128)(2,1)}), bf16[128,32,128]{0,2,1:T(8,128)(2,1)S(1)}, u32[]{:S(2)}, u32[]{:S(2)}) %all-to-all-start.1) | async-done | bytes 1048608 | tf_op jit(solution)/shard_map/all_to_all | solution.py:71
  61.6 1.0 copy-done.2
  62.6 1.6 copy.31
  64.2 31.1 %while.45 = (s32[]{:T(128)}, f32[1,4,1024]{2,1,0:T(4,128)S(1)}, f32[1,4,1024]{2,1,0:T(4,128)S(1)}, f32[1,4,1024,128]{3,2,1,0:T(8,128)S(1)}, bf16[4,256,1,128]{3,...) while((s32[]{:T(128)}, f32[1,4,1024]{2,1,0:T(4,128)S(1)}, ...), condition=%wide.region_3.4_spmd.clone, body=%wide.region_0.3_spmd.clone.sunk | while | flops 546856960 | bytes 34997380 | solution.py:47
  64.2 3.5 %bitcast_reduce_fusion.8 = (f32[4,1024]{1,0:T(4,128)S(1)}, f32[256,1024,4]{1,0,2:T(8,128)}) fusion(bf16[1024,1,4,128]{3,0,2,1:T(8,128)(2,1)S(1)} %get-tuple-element.409, bf16[4,256,1,128]{3,1,2,0:T(8,128)(2,1)} %get-tuple-element.408, s32[]{:T(128)} %get-tuple-element.395), kind=kOutput, calls=%fused_computation.55.clone.1 | convolution fusion | flops 270528512 | bytes 5325312 | tf_op jit(solution)/shard_map/while/body/eval_jaxpr/qgrd,kgd->grqk/dot_general | solution.py:30
  67.7 3.3 %bitcast_add_fusion.17 = f32[1,4,1024,128]{3,2,1,0:T(8,128)S(1)} fusion(f32[1,4,1024,128]{3,2,1,0:T(8,128)S(1)} %get-tuple-element.398, f32[256,1024,4]{1,0,2:T(8,128)} %get-tuple-element.384, f32[4,1024]{1,0:T(4,128)S(1)} %bitcast.252, f32[4,1024]{1,0:T(4,128)S(1)} %get-tuple-element.385, pred[]{:T(512)S(6)} %compare.3, ...), kind=kOutput, calls=%fused_computation.61.clone.1 | convolution fusion | flops 273154048 | bytes 8487425 | tf_op jit(solution)/shard_map/while/body/eval_jaxpr/grqk,kgd->grqd/dot_general | solution.py:38
  71.2 0.7 fusion.93
  72.0 3.5 %bitcast_reduce_fusion.8 = (f32[4,1024]{1,0:T(4,128)S(1)}, f32[256,1024,4]{1,0,2:T(8,128)}) fusion(bf16[1024,1,4,128]{3,0,2,1:T(8,128)(2,1)S(1)} %get-tuple-element.409, bf16[4,256,1,128]{3,1,2,0:T(8,128)(2,1)} %get-tuple-element.408, s32[]{:T(128)} %get-tuple-element.395), kind=kOutput, calls=%fused_computation.55.clone.1 | convolution fusion | flops 270528512 | bytes 5325312 | tf_op jit(solution)/shard_map/while/body/eval_jaxpr/qgrd,kgd->grqk/dot_general | solution.py:30
  75.5 3.3 %bitcast_add_fusion.17 = f32[1,4,1024,128]{3,2,1,0:T(8,128)S(1)} fusion(f32[1,4,1024,128]{3,2,1,0:T(8,128)S(1)} %get-tuple-element.398, f32[256,1024,4]{1,0,2:T(8,128)} %get-tuple-element.384, f32[4,1024]{1,0:T(4,128)S(1)} %bitcast.252, f32[4,1024]{1,0:T(4,128)S(1)} %get-tuple-element.385, pred[]{:T(512)S(6)} %compare.3, ...), kind=kOutput, calls=%fused_computation.61.clone.1 | convolution fusion | flops 273154048 | bytes 8487425 | tf_op jit(solution)/shard_map/while/body/eval_jaxpr/grqk,kgd->grqd/dot_general | solution.py:38
  78.8 0.2 copy-done.1
  79.0 0.7 fusion.93
  79.7 3.5 %bitcast_reduce_fusion.8 = (f32[4,1024]{1,0:T(4,128)S(1)}, f32[256,1024,4]{1,0,2:T(8,128)}) fusion(bf16[1024,1,4,128]{3,0,2,1:T(8,128)(2,1)S(1)} %get-tuple-element.409, bf16[4,256,1,128]{3,1,2,0:T(8,128)(2,1)} %get-tuple-element.408, s32[]{:T(128)} %get-tuple-element.395), kind=kOutput, calls=%fused_computation.55.clone.1 | convolution fusion | flops 270528512 | bytes 5325312 | tf_op jit(solution)/shard_map/while/body/eval_jaxpr/qgrd,kgd->grqk/dot_general | solution.py:30
  83.3 3.3 %bitcast_add_fusion.17 = f32[1,4,1024,128]{3,2,1,0:T(8,128)S(1)} fusion(f32[1,4,1024,128]{3,2,1,0:T(8,128)S(1)} %get-tuple-element.398, f32[256,1024,4]{1,0,2:T(8,128)} %get-tuple-element.384, f32[4,1024]{1,0:T(4,128)S(1)} %bitcast.252, f32[4,1024]{1,0:T(4,128)S(1)} %get-tuple-element.385, pred[]{:T(512)S(6)} %compare.3, ...), kind=kOutput, calls=%fused_computation.61.clone.1 | convolution fusion | flops 273154048 | bytes 8487425 | tf_op jit(solution)/shard_map/while/body/eval_jaxpr/grqk,kgd->grqd/dot_general | solution.py:38
  86.6 0.2 copy-done.1
  86.7 0.7 fusion.93
  87.5 3.5 %bitcast_reduce_fusion.8 = (f32[4,1024]{1,0:T(4,128)S(1)}, f32[256,1024,4]{1,0,2:T(8,128)}) fusion(bf16[1024,1,4,128]{3,0,2,1:T(8,128)(2,1)S(1)} %get-tuple-element.409, bf16[4,256,1,128]{3,1,2,0:T(8,128)(2,1)} %get-tuple-element.408, s32[]{:T(128)} %get-tuple-element.395), kind=kOutput, calls=%fused_computation.55.clone.1 | convolution fusion | flops 270528512 | bytes 5325312 | tf_op jit(solution)/shard_map/while/body/eval_jaxpr/qgrd,kgd->grqk/dot_general | solution.py:30
  91.0 3.3 %bitcast_add_fusion.17 = f32[1,4,1024,128]{3,2,1,0:T(8,128)S(1)} fusion(f32[1,4,1024,128]{3,2,1,0:T(8,128)S(1)} %get-tuple-element.398, f32[256,1024,4]{1,0,2:T(8,128)} %get-tuple-element.384, f32[4,1024]{1,0:T(4,128)S(1)} %bitcast.252, f32[4,1024]{1,0:T(4,128)S(1)} %get-tuple-element.385, pred[]{:T(512)S(6)} %compare.3, ...), kind=kOutput, calls=%fused_computation.61.clone.1 | convolution fusion | flops 273154048 | bytes 8487425 | tf_op jit(solution)/shard_map/while/body/eval_jaxpr/grqk,kgd->grqd/dot_general | solution.py:38
  94.3 0.2 copy-done.1
  94.5 0.7 fusion.93
  95.3 20.8 %while.43 = (s32[]{:T(128)}, f32[1,4,1024]{2,1,0:T(4,128)S(1)}, f32[1,4,1024]{2,1,0:T(4,128)S(1)}, f32[1,4,1024,128]{3,2,1,0:T(8,128)S(1)}, pred[]{:T(512)}, /*i...) while((s32[]{:T(128)}, f32[1,4,1024]{2,1,0:T(4,128)S(1)}, ...), condition=%wide.region_7.8_spmd, body=%wide.region_4.7_spmd.sunk | while | flops 549466112 | bytes 18221148 | solution.py:47
  95.3 1.6 bitcast_reduce_fusion.6
  96.9 2.7 %bitcast_add_fusion.13 = f32[1,4,1024,128]{3,2,1,0:T(8,128)S(1)} fusion(f32[1,4,1024,128]{3,2,1,0:T(8,128)S(1)} %get-tuple-element.425, f32[256,1024,4]{1,0,2:T(8,128)S(1)} %get-tuple-element.361, f32[4,1024]{1,0:T(4,128)S(1)} %bitcast.254, pred[]{:T(512)} %get-tuple-element.435, f32[4,1024]{1,0:T(4,128)S(1)} %get-tuple-element.362, ...), kind=kOutput, calls=%fused_computation.8.clone.1 | convolution fusion | flops 273678336 | bytes 8487936 | tf_op jit(solution)/shard_map/while/body/eval_jaxpr/grqk,kgd->grqd/dot_general | solution.py:38
  99.6 0.9 fusion.85
  100.5 1.6 bitcast_reduce_fusion.6
  102.1 2.7 %bitcast_add_fusion.13 = f32[1,4,1024,128]{3,2,1,0:T(8,128)S(1)} fusion(f32[1,4,1024,128]{3,2,1,0:T(8,128)S(1)} %get-tuple-element.425, f32[256,1024,4]{1,0,2:T(8,128)S(1)} %get-tuple-element.361, f32[4,1024]{1,0:T(4,128)S(1)} %bitcast.254, pred[]{:T(512)} %get-tuple-element.435, f32[4,1024]{1,0:T(4,128)S(1)} %get-tuple-element.362, ...), kind=kOutput, calls=%fused_computation.8.clone.1 | convolution fusion | flops 273678336 | bytes 8487936 | tf_op jit(solution)/shard_map/while/body/eval_jaxpr/grqk,kgd->grqd/dot_general | solution.py:38
  104.8 0.9 fusion.85
  105.7 1.6 bitcast_reduce_fusion.6
  107.3 2.7 %bitcast_add_fusion.13 = f32[1,4,1024,128]{3,2,1,0:T(8,128)S(1)} fusion(f32[1,4,1024,128]{3,2,1,0:T(8,128)S(1)} %get-tuple-element.425, f32[256,1024,4]{1,0,2:T(8,128)S(1)} %get-tuple-element.361, f32[4,1024]{1,0:T(4,128)S(1)} %bitcast.254, pred[]{:T(512)} %get-tuple-element.435, f32[4,1024]{1,0:T(4,128)S(1)} %get-tuple-element.362, ...), kind=kOutput, calls=%fused_computation.8.clone.1 | convolution fusion | flops 273678336 | bytes 8487936 | tf_op jit(solution)/shard_map/while/body/eval_jaxpr/grqk,kgd->grqd/dot_general | solution.py:38
  110.0 0.9 fusion.85
  110.9 1.6 bitcast_reduce_fusion.6
  112.5 2.7 %bitcast_add_fusion.13 = f32[1,4,1024,128]{3,2,1,0:T(8,128)S(1)} fusion(f32[1,4,1024,128]{3,2,1,0:T(8,128)S(1)} %get-tuple-element.425, f32[256,1024,4]{1,0,2:T(8,128)S(1)} %get-tuple-element.361, f32[4,1024]{1,0:T(4,128)S(1)} %bitcast.254, pred[]{:T(512)} %get-tuple-element.435, f32[4,1024]{1,0:T(4,128)S(1)} %get-tuple-element.362, ...), kind=kOutput, calls=%fused_computation.8.clone.1 | convolution fusion | flops 273678336 | bytes 8487936 | tf_op jit(solution)/shard_map/while/body/eval_jaxpr/grqk,kgd->grqd/dot_general | solution.py:38
  115.2 0.9 fusion.85
  116.1 20.8 %while.44 = (s32[]{:T(128)}, f32[1,4,1024]{2,1,0:T(4,128)S(1)}, f32[1,4,1024]{2,1,0:T(4,128)S(1)}, f32[1,4,1024,128]{3,2,1,0:T(8,128)S(1)}, pred[]{:T(512)}, /*i...) while((s32[]{:T(128)}, f32[1,4,1024]{2,1,0:T(4,128)S(1)}, ...), condition=%wide.region_11.12_spmd, body=%wide.region_8.11_spmd.sunk | while | flops 549466112 | bytes 18221148 | solution.py:47
  116.1 1.6 bitcast_reduce_fusion.7
  117.7 2.7 %bitcast_add_fusion.15 = f32[1,4,1024,128]{3,2,1,0:T(8,128)S(1)} fusion(f32[1,4,1024,128]{3,2,1,0:T(8,128)S(1)} %get-tuple-element.452, f32[256,1024,4]{1,0,2:T(8,128)S(1)} %get-tuple-element.373, f32[4,1024]{1,0:T(4,128)S(1)} %bitcast.256, pred[]{:T(512)} %get-tuple-element.462, f32[4,1024]{1,0:T(4,128)S(1)} %get-tuple-element.374, ...), kind=kOutput, calls=%fused_computation.35.clone.1 | convolution fusion | flops 273678336 | bytes 8487936 | tf_op jit(solution)/shard_map/while/body/eval_jaxpr/grqk,kgd->grqd/dot_general | solution.py:38
  120.4 0.9 fusion.89
  121.3 1.6 bitcast_reduce_fusion.7
  122.9 2.7 %bitcast_add_fusion.15 = f32[1,4,1024,128]{3,2,1,0:T(8,128)S(1)} fusion(f32[1,4,1024,128]{3,2,1,0:T(8,128)S(1)} %get-tuple-element.452, f32[256,1024,4]{1,0,2:T(8,128)S(1)} %get-tuple-element.373, f32[4,1024]{1,0:T(4,128)S(1)} %bitcast.256, pred[]{:T(512)} %get-tuple-element.462, f32[4,1024]{1,0:T(4,128)S(1)} %get-tuple-element.374, ...), kind=kOutput, calls=%fused_computation.35.clone.1 | convolution fusion | flops 273678336 | bytes 8487936 | tf_op jit(solution)/shard_map/while/body/eval_jaxpr/grqk,kgd->grqd/dot_general | solution.py:38
  125.6 0.9 fusion.89
  126.5 1.6 bitcast_reduce_fusion.7
  128.1 2.7 %bitcast_add_fusion.15 = f32[1,4,1024,128]{3,2,1,0:T(8,128)S(1)} fusion(f32[1,4,1024,128]{3,2,1,0:T(8,128)S(1)} %get-tuple-element.452, f32[256,1024,4]{1,0,2:T(8,128)S(1)} %get-tuple-element.373, f32[4,1024]{1,0:T(4,128)S(1)} %bitcast.256, pred[]{:T(512)} %get-tuple-element.462, f32[4,1024]{1,0:T(4,128)S(1)} %get-tuple-element.374, ...), kind=kOutput, calls=%fused_computation.35.clone.1 | convolution fusion | flops 273678336 | bytes 8487936 | tf_op jit(solution)/shard_map/while/body/eval_jaxpr/grqk,kgd->grqd/dot_general | solution.py:38
  130.8 0.9 fusion.89
  131.7 1.6 bitcast_reduce_fusion.7
  133.3 2.7 %bitcast_add_fusion.15 = f32[1,4,1024,128]{3,2,1,0:T(8,128)S(1)} fusion(f32[1,4,1024,128]{3,2,1,0:T(8,128)S(1)} %get-tuple-element.452, f32[256,1024,4]{1,0,2:T(8,128)S(1)} %get-tuple-element.373, f32[4,1024]{1,0:T(4,128)S(1)} %bitcast.256, pred[]{:T(512)} %get-tuple-element.462, f32[4,1024]{1,0:T(4,128)S(1)} %get-tuple-element.374, ...), kind=kOutput, calls=%fused_computation.35.clone.1 | convolution fusion | flops 273678336 | bytes 8487936 | tf_op jit(solution)/shard_map/while/body/eval_jaxpr/grqk,kgd->grqd/dot_general | solution.py:38
  136.0 0.9 fusion.89
  136.9 0.2 copy.33
  137.2 6.5 %fusion.67 = bf16[1024,4,128]{2,1,0:T(4,128)(2,1)S(1)} fusion(f32[4,1024]{0,1:T(8,128)S(1)} %copy.33, f32[1,4,1024,128]{3,2,1,0:T(8,128)S(1)} %get-tuple-element.137), kind=kLoop, calls=%fused_computation.81 | loop fusion | flops 1048576 | bytes 3162112 | tf_op jit(solution)/shard_map/transpose | solution.py:84
  143.7 29.0 %all_to_all.66 = bf16[1024,4,128]{2,1,0:T(4,128)(2,1)S(1)} all-to-all(bf16[1024,4,128]{2,1,0:T(4,128)(2,1)S(1)} %fusion.67), channel_id=1, replica_groups=mesh['outer'=4,'inner'=8] {'inner'}, dimensions={0} | all-to-all | bytes 2097152 | tf_op jit(solution)/shard_map/all_to_all | solution.py:85
  172.7 0.4 copy.35
  173.1 1.6 reshape.130
  (53 shorter events, 0.7 us)
Async XLA Ops:
  0.0 1.0 copy-start
  1.7 16.1 %all-to-all-start = ((bf16[128,8,128]{2,0,1:T(8,128)(2,1)}), bf16[128,8,128]{2,0,1:T(8,128)(2,1)S(1)}, u32[]{:S(2)}, u32[]{:S(2)}) async-start(bf16[128,8,128]{2,0,1:T(8,128)(2,1)} %copy_bitcast_fusion.1), calls=%async_computation | async-start | bytes 524288 | tf_op jit(solution)/shard_map/all_to_all | solution.py:72
  17.8 13.1 %copy-start.3 = (bf16[128,8,128]{2,0,1:T(8,128)(2,1)}, bf16[128,8,128]{2,0,1:T(8,128)(2,1)S(1)}, u32[]{:S(2)}) copy-start(bf16[128,8,128]{2,0,1:T(8,128)(2,1)S(1)} %all-to-all-done) | copy-start | bytes 786436
  17.8 13.1 %all-to-all-start.2 = ((bf16[128,8,128]{2,0,1:T(8,128)(2,1)}), bf16[128,8,128]{2,0,1:T(8,128)(2,1)S(1)}, u32[]{:S(2)}, u32[]{:S(2)}) async-start(bf16[128,8,128]{2,0,1:T(8,128)(2,1)} %copy_bitcast_fusion), calls=%async_computation.2 | async-start | bytes 524288 | tf_op jit(solution)/shard_map/all_to_all | solution.py:73
  30.8 0.7 copy-start.4
  31.5 30.1 %all-to-all-start.1 = ((bf16[128,32,128]{0,2,1:T(8,128)(2,1)}), bf16[128,32,128]{0,2,1:T(8,128)(2,1)S(1)}, u32[]{:S(2)}, u32[]{:S(2)}) async-start(bf16[128,32,128]{0,2,1:T(8,128)(2,1)} %bitcast.31), calls=%async_computation.1 | async-start | bytes 2097152 | tf_op jit(solution)/shard_map/all_to_all | solution.py:71
  35.1 60.1 %collective-permute-start = (bf16[1024,1,128]{2,0,1:T(8,128)(2,1)}, bf16[1024,1,128]{2,0,1:T(8,128)(2,1)}, u32[]{:S(2)}, u32[]{:S(2)}) collective-permute-start(bf16[1024,1,128]{2,0,1:T(8,128)(2,1)} %bitcast.261), channel_id=1, source_target_pairs={{0,8},{8,16},{16,24},{1,9},{9,17},{17,25},{2,10},{10,18},{18,26},{... | collective-permute-start | bytes 786440 | tf_op jit(solution)/shard_map/ppermute | solution.py:14
  39.3 76.8 %collective-permute-start.2 = (bf16[1024,1,128]{2,0,1:T(8,128)(2,1)}, bf16[1024,1,128]{2,0,1:T(8,128)(2,1)}, u32[]{:S(2)}, u32[]{:S(2)}) collective-permute-start(bf16[1024,1,128]{2,0,1:T(8,128)(2,1)} %bitcast.262), channel_id=1, source_target_pairs={{8,0},{16,8},{24,16},{9,1},{17,9},{25,17},{10,2},{18,10},{26,18},{... | collective-permute-start | bytes 786440 | tf_op jit(solution)/shard_map/ppermute | solution.py:14
  40.5 54.7 %collective-permute-start.1 = (bf16[1024,1,128]{2,0,1:T(8,128)(2,1)}, bf16[1024,1,128]{2,0,1:T(8,128)(2,1)}, u32[]{:S(2)}, u32[]{:S(2)}) collective-permute-start(bf16[1024,1,128]{2,0,1:T(8,128)(2,1)} %bitcast.264), channel_id=1, source_target_pairs={{0,8},{8,16},{16,24},{1,9},{9,17},{17,25},{2,10},{10,18},{18,26},{... | collective-permute-start | bytes 786440 | tf_op jit(solution)/shard_map/ppermute | solution.py:14
  45.8 70.3 %collective-permute-start.3 = (bf16[1024,1,128]{2,0,1:T(8,128)(2,1)}, bf16[1024,1,128]{2,0,1:T(8,128)(2,1)}, u32[]{:S(2)}, u32[]{:S(2)}) collective-permute-start(bf16[1024,1,128]{2,0,1:T(8,128)(2,1)} %bitcast.265), channel_id=1, source_target_pairs={{8,0},{16,8},{24,16},{9,1},{17,9},{25,17},{10,2},{18,10},{26,18},{... | collective-permute-start | bytes 786440 | tf_op jit(solution)/shard_map/ppermute | solution.py:14
  61.6 1.0 copy-start.2
  67.7 3.5 %copy-start.1 = (f32[256,1024,4]{1,0,2:T(8,128)S(1)}, f32[256,1024,4]{1,0,2:T(8,128)}, u32[]{:S(2)}) copy-start(f32[256,1024,4]{1,0,2:T(8,128)} %get-tuple-element.384) | copy-start | bytes 12582916 | tf_op jit(solution)/shard_map/while
  75.5 3.5 %copy-start.1 = (f32[256,1024,4]{1,0,2:T(8,128)S(1)}, f32[256,1024,4]{1,0,2:T(8,128)}, u32[]{:S(2)}) copy-start(f32[256,1024,4]{1,0,2:T(8,128)} %get-tuple-element.384) | copy-start | bytes 12582916 | tf_op jit(solution)/shard_map/while
  83.3 3.5 %copy-start.1 = (f32[256,1024,4]{1,0,2:T(8,128)S(1)}, f32[256,1024,4]{1,0,2:T(8,128)}, u32[]{:S(2)}) copy-start(f32[256,1024,4]{1,0,2:T(8,128)} %get-tuple-element.384) | copy-start | bytes 12582916 | tf_op jit(solution)/shard_map/while
  91.0 3.5 %copy-start.1 = (f32[256,1024,4]{1,0,2:T(8,128)S(1)}, f32[256,1024,4]{1,0,2:T(8,128)}, u32[]{:S(2)}) copy-start(f32[256,1024,4]{1,0,2:T(8,128)} %get-tuple-element.384) | copy-start | bytes 12582916 | tf_op jit(solution)/shard_map/while
where the time goes:
time: 176 us; the launch traced here: 175 us
  matrix products  61.1 us (35%)
  waiting for transfers between devices  29.9 us (17%)
  blocking collectives  29 us (16%)
  starting transfers between devices  25.3 us (14%)
  other arithmetic  16.8 us (10%)
  local copies, waits for them, and re-layouts  11.9 us (7%)
    dot_general x12, matrix products, one_block(): jnp.einsum('grqk,kgd->grqd', weights.astype(jnp.bfloat16), value_block, p...  34.6 us
    all_to_all x1, blocking collectives, shards(): lax.all_to_all(mixed, 'inner', split_axis=0, concat_axis=1, tiled=True)  29 us
    dot_general x12, matrix products, one_block(): jnp.einsum('qgrd,kgd->grqk', grouped, key_block, preferred_element_type=j...  26.5 us
    all_to_all x1, waiting for transfers between devices, shards(): lax.all_to_all(query_heads, 'inner', split_axis=1, concat_axis=0, tiled=T...  14.5 us
    ppermute x4, starting transfers between devices, shifted(): return lax.ppermute(block, axis, route)  11.9 us
    reduce_sum x12, other arithmetic, one_block(): total = total * factor + jnp.sum(weights, axis=-1)  9.77 us
    all_to_all x1, waiting for transfers between devices, shards(): lax.all_to_all(key_heads, 'inner', split_axis=1, concat_axis=0, tiled=True)  8.01 us
    all_to_all x1, waiting for transfers between devices, shards(): lax.all_to_all(value_heads, 'inner', split_axis=1, concat_axis=0, tiled=T...  7.37 us
  transfers between devices with their start and end apart: 7, of which 3 were waited for; matrix products, arithmetic and copies ran while one was open for 32% of the time, Pallas kernels for 0%

commit v1 on v0

--- a/solution.py
+++ b/solution.py
@@ -57,6 +57,24 @@
 
 
 def shards(queries, keys, values):
+
+    def change_islands_by_axis(matrix):
+        device_axis = "inner"
+        o_now, far_arr = (lax.psum(1, device_axis), lax.axis_index(device_axis))
+        near = matrix.shape[0] // o_now
+        val = jnp.roll(matrix, -far_arr * near, axis=0)
+        heap = [lax.slice_in_dim(val, 0, near, axis=0)]
+        for i0 in range(1, o_now):
+            e_next = lax.slice_in_dim(val, i0 * near, (i0 + 1) * near, axis=0)
+            heap.append(
+                lax.ppermute(
+                    e_next, device_axis, [(src_i, (src_i + i0) % o_now) for src_i in range(o_now)]
+                )
+            )
+        step_out = jnp.concatenate(heap[::-1], axis=1)
+        x_now = jnp.roll(step_out, (far_arr + 1) * heap[0].shape[1], axis=1)
+        return x_now
+
     tokens = queries.shape[0]
     position = lax.axis_index("outer")
     before_ok = position > 0
@@ -82,7 +100,7 @@
     peak, total, accum = state
     mixed = (accum / total[..., None]).astype(jnp.bfloat16)
     mixed = mixed.reshape(per_device, rows, HD).transpose(1, 0, 2)
-    back = lax.all_to_all(mixed, "inner", split_axis=0, concat_axis=1, tiled=True)
+    back = change_islands_by_axis(mixed)
     return back.reshape(tokens, QH * HD)
 
 

time: 176 us -> 166 us (0.943)
  blocking collectives: 29 us -> 0 us
  waiting for transfers between devices: 29.9 us -> 50.5 us
  other arithmetic: 16.8 us -> 11.9 us
  starting transfers between devices: 25.3 us -> 29.4 us
    all_to_all x1 -> x0, blocking collectives: 29 us -> none  [shards(): lax.all_to_all(mixed, 'inner', split_axis=0, concat_axis=1, tiled=True)]
    ppermute x0 -> x7, waiting for transfers between devices: none -> 19.7 us  [change_islands_by_axis(): lax.ppermute(e_next, device_axis, [(src_i, (src_i + i0) % o_now) for src_...]
    transpose x1, other arithmetic: 6.53 us -> 0.73 us  [shards(): mixed = mixed.reshape(per_device, rows, HD).transpose(1, 0, 2)]
    ppermute x0 -> x7, starting transfers between devices: none -> 4.16 us  [change_islands_by_axis(): lax.ppermute(e_next, device_axis, [(src_i, (src_i + i0) % o_now) for src_...]
    unnamed x9 -> x26, local copies, waits for them, and re-layouts: 4.9 us -> 4.22 us
  transfers between devices with their start and end apart: 7 -> 14, of which waited for: 3 -> 8; matrix products, arithmetic and copies ran while one was open for 32% -> 34% of each run, Pallas kernels for 0% -> 0%
where the time goes in v1:
time: 166 us; the launch traced here: 164 us
  matrix products  61.1 us (37%)
  waiting for transfers between devices  50.5 us (30%)
  starting transfers between devices  29.4 us (18%)
  other arithmetic  11.9 us (7%)
  local copies, waits for them, and re-layouts  10.3 us (6%)
    dot_general x12, matrix products, one_block(): jnp.einsum('grqk,kgd->grqd', weights.astype(jnp.bfloat16), value_block, p...  34.6 us
    dot_general x12, matrix products, one_block(): jnp.einsum('qgrd,kgd->grqk', grouped, key_block, preferred_element_type=j...  26.6 us
    ppermute x7, waiting for transfers between devices, change_islands_by_axis(): lax.ppermute(e_next, device_axis, [(src_i, (src_i + i0) % o_now) for src_...  19.7 us
    all_to_all x1, waiting for transfers between devices, shards(): lax.all_to_all(query_heads, 'inner', split_axis=1, concat_axis=0, tiled=T...  14.5 us
    ppermute x4, starting transfers between devices, shifted(): return lax.ppermute(block, axis, route)  11.9 us
    reduce_sum x12, other arithmetic, one_block(): total = total * factor + jnp.sum(weights, axis=-1)  9.77 us
    all_to_all x1, waiting for transfers between devices, shards(): lax.all_to_all(value_heads, 'inner', split_axis=1, concat_axis=0, tiled=T...  8.32 us
    all_to_all x1, waiting for transfers between devices, shards(): lax.all_to_all(key_heads, 'inner', split_axis=1, concat_axis=0, tiled=True)  8.01 us
  transfers between devices with their start and end apart: 14, of which 8 were waited for; matrix products, arithmetic and copies ran while one was open for 34% of the time, Pallas kernels for 0%

profile of v1, /device:TPU:0, one launch (start us, length us, event | category | flops | bytes accessed | tf_op | source)
XLA Modules:
  0.0 164.1 jit_solution(15049226792871771350)
XLA Ops:
  0.0 0.9 copy-done
  1.0 0.8 copy_bitcast_fusion.2
  1.7 6.4 %all-to-all-start = ((bf16[128,8,128]{2,0,1:T(8,128)(2,1)}), bf16[128,8,128]{2,0,1:T(8,128)(2,1)S(1)}, u32[]{:S(2)}, u32[]{:S(2)}) async-start(bf16[128,8,128]{2,0,1:T(8,128)(2,1)} %copy_bitcast_fusion.2), calls=%async_computation | async-start | bytes 524288 | tf_op jit(solution)/shard_map/all_to_all | solution.py:90
  8.1 1.7 %copy_bitcast_fusion.1 = bf16[128,8,128]{2,0,1:T(8,128)(2,1)} fusion(bf16[128,1024]{1,0:T(8,128)(2,1)} %param.11), kind=kLoop, calls=%fused_computation.86 | loop fusion | bytes 524288 | tf_op jit(solution)/shard_map/reshape;broadcast_in_dim;reshape | solution.py:87
  9.8 8.0 %all-to-all-done = bf16[128,8,128]{2,0,1:T(8,128)(2,1)S(1)} async-done(((bf16[128,8,128]{2,0,1:T(8,128)(2,1)}), bf16[128,8,128]{2,0,1:T(8,128)(2,1)S(1)}, u32[]{:S(2)}, u32[]{:S(2)}) %all-to-all-start) | async-done | bytes 262176 | tf_op jit(solution)/shard_map/all_to_all | solution.py:90
  17.8 3.4 %all-to-all-start.2 = ((bf16[128,8,128]{2,0,1:T(8,128)(2,1)}), bf16[128,8,128]{2,0,1:T(8,128)(2,1)S(1)}, u32[]{:S(2)}, u32[]{:S(2)}) async-start(bf16[128,8,128]{2,0,1:T(8,128)(2,1)} %copy_bitcast_fusion.1), calls=%async_computation.2 | async-start | bytes 524288 | tf_op jit(solution)/shard_map/all_to_all | solution.py:91
  21.2 1.3 copy.20
  22.5 8.3 %all-to-all-done.2 = bf16[128,8,128]{2,0,1:T(8,128)(2,1)S(1)} async-done(((bf16[128,8,128]{2,0,1:T(8,128)(2,1)}), bf16[128,8,128]{2,0,1:T(8,128)(2,1)S(1)}, u32[]{:S(2)}, u32[]{:S(2)}) %all-to-all-start.2) | async-done | bytes 262176 | tf_op jit(solution)/shard_map/all_to_all | solution.py:91
  31.5 3.6 %all-to-all-start.1 = ((bf16[128,32,128]{0,2,1:T(8,128)(2,1)}), bf16[128,32,128]{0,2,1:T(8,128)(2,1)S(1)}, u32[]{:S(2)}, u32[]{:S(2)}) async-start(bf16[128,32,128]{0,2,1:T(8,128)(2,1)} %bitcast.31), calls=%async_computation.1 | async-start | bytes 2097152 | tf_op jit(solution)/shard_map/all_to_all | solution.py:89
  35.2 4.1 %collective-permute-start = (bf16[1024,1,128]{2,0,1:T(8,128)(2,1)}, bf16[1024,1,128]{2,0,1:T(8,128)(2,1)}, u32[]{:S(2)}, u32[]{:S(2)}) collective-permute-start(bf16[1024,1,128]{2,0,1:T(8,128)(2,1)} %bitcast.262), channel_id=1, source_target_pairs={{0,8},{8,16},{16,24},{1,9},{9,17},{17,25},{2,10},{10,18},{18,26},{... | collective-permute-start | bytes 786440 | tf_op jit(solution)/shard_map/ppermute | solution.py:14
  39.3 1.3 collective-permute-start.2
  40.6 5.3 %collective-permute-start.1 = (bf16[1024,1,128]{2,0,1:T(8,128)(2,1)}, bf16[1024,1,128]{2,0,1:T(8,128)(2,1)}, u32[]{:S(2)}, u32[]{:S(2)}) collective-permute-start(bf16[1024,1,128]{2,0,1:T(8,128)(2,1)} %bitcast.265), channel_id=1, source_target_pairs={{0,8},{8,16},{16,24},{1,9},{9,17},{17,25},{2,10},{10,18},{18,26},{... | collective-permute-start | bytes 786440 | tf_op jit(solution)/shard_map/ppermute | solution.py:14
  45.8 1.3 collective-permute-start.3
  47.1 14.5 %all-to-all-done.1 = bf16[128,32,128]{0,2,1:T(8,128)(2,1)S(1)} async-done(((bf16[128,32,128]{0,2,1:T(8,128)(2,1)}), bf16[128,32,128]{0,2,1:T(8,128)(2,1)S(1)}, u32[]{:S(2)}, u32[]{:S(2)}) %all-to-all-start.1) | async-done | bytes 1048608 | tf_op jit(solution)/shard_map/all_to_all | solution.py:89
  61.6 1.0 copy-done.2
  62.6 1.6 copy.22
  64.2 31.1 %while.45 = (s32[]{:T(128)}, f32[1,4,1024]{2,1,0:T(4,128)S(1)}, f32[1,4,1024]{2,1,0:T(4,128)S(1)}, f32[1,4,1024,128]{3,2,1,0:T(8,128)S(1)}, bf16[4,256,1,128]{3,...) while((s32[]{:T(128)}, f32[1,4,1024]{2,1,0:T(4,128)S(1)}, ...), condition=%wide.region_3.4_spmd.clone, body=%wide.region_0.3_spmd.clone.sunk | while | flops 546856960 | bytes 34997380 | solution.py:47
  64.2 3.5 %bitcast_reduce_fusion.8 = (f32[4,1024]{1,0:T(4,128)S(1)}, f32[256,1024,4]{1,0,2:T(8,128)}) fusion(bf16[1024,1,4,128]{3,0,2,1:T(8,128)(2,1)S(1)} %get-tuple-element.416, bf16[4,256,1,128]{3,1,2,0:T(8,128)(2,1)} %get-tuple-element.415, s32[]{:T(128)} %get-tuple-element.402), kind=kOutput, calls=%fused_computation.55.clone.1 | convolution fusion | flops 270528512 | bytes 5325312 | tf_op jit(solution)/shard_map/while/body/eval_jaxpr/qgrd,kgd->grqk/dot_general | solution.py:30
  67.7 3.3 %bitcast_add_fusion.17 = f32[1,4,1024,128]{3,2,1,0:T(8,128)S(1)} fusion(f32[1,4,1024,128]{3,2,1,0:T(8,128)S(1)} %get-tuple-element.405, f32[256,1024,4]{1,0,2:T(8,128)} %get-tuple-element.391, f32[4,1024]{1,0:T(4,128)S(1)} %bitcast.254, f32[4,1024]{1,0:T(4,128)S(1)} %get-tuple-element.392, pred[]{:T(512)S(6)} %compare.5, ...), kind=kOutput, calls=%fused_computation.61.clone.1 | convolution fusion | flops 273154048 | bytes 8487425 | tf_op jit(solution)/shard_map/while/body/eval_jaxpr/grqk,kgd->grqd/dot_general | solution.py:38
  71.2 0.7 fusion.94
  72.0 3.5 %bitcast_reduce_fusion.8 = (f32[4,1024]{1,0:T(4,128)S(1)}, f32[256,1024,4]{1,0,2:T(8,128)}) fusion(bf16[1024,1,4,128]{3,0,2,1:T(8,128)(2,1)S(1)} %get-tuple-element.416, bf16[4,256,1,128]{3,1,2,0:T(8,128)(2,1)} %get-tuple-element.415, s32[]{:T(128)} %get-tuple-element.402), kind=kOutput, calls=%fused_computation.55.clone.1 | convolution fusion | flops 270528512 | bytes 5325312 | tf_op jit(solution)/shard_map/while/body/eval_jaxpr/qgrd,kgd->grqk/dot_general | solution.py:30
  75.5 3.3 %bitcast_add_fusion.17 = f32[1,4,1024,128]{3,2,1,0:T(8,128)S(1)} fusion(f32[1,4,1024,128]{3,2,1,0:T(8,128)S(1)} %get-tuple-element.405, f32[256,1024,4]{1,0,2:T(8,128)} %get-tuple-element.391, f32[4,1024]{1,0:T(4,128)S(1)} %bitcast.254, f32[4,1024]{1,0:T(4,128)S(1)} %get-tuple-element.392, pred[]{:T(512)S(6)} %compare.5, ...), kind=kOutput, calls=%fused_computation.61.clone.1 | convolution fusion | flops 273154048 | bytes 8487425 | tf_op jit(solution)/shard_map/while/body/eval_jaxpr/grqk,kgd->grqd/dot_general | solution.py:38
  79.0 0.7 fusion.94
  79.8 3.5 %bitcast_reduce_fusion.8 = (f32[4,1024]{1,0:T(4,128)S(1)}, f32[256,1024,4]{1,0,2:T(8,128)}) fusion(bf16[1024,1,4,128]{3,0,2,1:T(8,128)(2,1)S(1)} %get-tuple-element.416, bf16[4,256,1,128]{3,1,2,0:T(8,128)(2,1)} %get-tuple-element.415, s32[]{:T(128)} %get-tuple-element.402), kind=kOutput, calls=%fused_computation.55.clone.1 | convolution fusion | flops 270528512 | bytes 5325312 | tf_op jit(solution)/shard_map/while/body/eval_jaxpr/qgrd,kgd->grqk/dot_general | solution.py:30
  83.3 3.3 %bitcast_add_fusion.17 = f32[1,4,1024,128]{3,2,1,0:T(8,128)S(1)} fusion(f32[1,4,1024,128]{3,2,1,0:T(8,128)S(1)} %get-tuple-element.405, f32[256,1024,4]{1,0,2:T(8,128)} %get-tuple-element.391, f32[4,1024]{1,0:T(4,128)S(1)} %bitcast.254, f32[4,1024]{1,0:T(4,128)S(1)} %get-tuple-element.392, pred[]{:T(512)S(6)} %compare.5, ...), kind=kOutput, calls=%fused_computation.61.clone.1 | convolution fusion | flops 273154048 | bytes 8487425 | tf_op jit(solution)/shard_map/while/body/eval_jaxpr/grqk,kgd->grqd/dot_general | solution.py:38
  87.5 3.5 %bitcast_reduce_fusion.8 = (f32[4,1024]{1,0:T(4,128)S(1)}, f32[256,1024,4]{1,0,2:T(8,128)}) fusion(bf16[1024,1,4,128]{3,0,2,1:T(8,128)(2,1)S(1)} %get-tuple-element.416, bf16[4,256,1,128]{3,1,2,0:T(8,128)(2,1)} %get-tuple-element.415, s32[]{:T(128)} %get-tuple-element.402), kind=kOutput, calls=%fused_computation.55.clone.1 | convolution fusion | flops 270528512 | bytes 5325312 | tf_op jit(solution)/shard_map/while/body/eval_jaxpr/qgrd,kgd->grqk/dot_general | solution.py:30
  91.1 3.3 %bitcast_add_fusion.17 = f32[1,4,1024,128]{3,2,1,0:T(8,128)S(1)} fusion(f32[1,4,1024,128]{3,2,1,0:T(8,128)S(1)} %get-tuple-element.405, f32[256,1024,4]{1,0,2:T(8,128)} %get-tuple-element.391, f32[4,1024]{1,0:T(4,128)S(1)} %bitcast.254, f32[4,1024]{1,0:T(4,128)S(1)} %get-tuple-element.392, pred[]{:T(512)S(6)} %compare.5, ...), kind=kOutput, calls=%fused_computation.61.clone.1 | convolution fusion | flops 273154048 | bytes 8487425 | tf_op jit(solution)/shard_map/while/body/eval_jaxpr/grqk,kgd->grqd/dot_general | solution.py:38
  94.5 0.7 fusion.94
  95.3 20.8 %while.43 = (s32[]{:T(128)}, f32[1,4,1024]{2,1,0:T(4,128)S(1)}, f32[1,4,1024]{2,1,0:T(4,128)S(1)}, f32[1,4,1024,128]{3,2,1,0:T(8,128)S(1)}, pred[]{:T(512)}, /*i...) while((s32[]{:T(128)}, f32[1,4,1024]{2,1,0:T(4,128)S(1)}, ...), condition=%wide.region_7.8_spmd, body=%wide.region_4.7_spmd.sunk | while | flops 549466112 | bytes 18221148 | solution.py:47
  95.3 1.6 bitcast_reduce_fusion.6
  96.9 2.7 %bitcast_add_fusion.13 = f32[1,4,1024,128]{3,2,1,0:T(8,128)S(1)} fusion(f32[1,4,1024,128]{3,2,1,0:T(8,128)S(1)} %get-tuple-element.432, f32[256,1024,4]{1,0,2:T(8,128)S(1)} %get-tuple-element.368, f32[4,1024]{1,0:T(4,128)S(1)} %bitcast.256, pred[]{:T(512)} %get-tuple-element.442, f32[4,1024]{1,0:T(4,128)S(1)} %get-tuple-element.369, ...), kind=kOutput, calls=%fused_computation.8.clone.1 | convolution fusion | flops 273678336 | bytes 8487936 | tf_op jit(solution)/shard_map/while/body/eval_jaxpr/grqk,kgd->grqd/dot_general | solution.py:38
  99.6 0.9 fusion.86
  100.5 1.6 bitcast_reduce_fusion.6
  102.1 2.7 %bitcast_add_fusion.13 = f32[1,4,1024,128]{3,2,1,0:T(8,128)S(1)} fusion(f32[1,4,1024,128]{3,2,1,0:T(8,128)S(1)} %get-tuple-element.432, f32[256,1024,4]{1,0,2:T(8,128)S(1)} %get-tuple-element.368, f32[4,1024]{1,0:T(4,128)S(1)} %bitcast.256, pred[]{:T(512)} %get-tuple-element.442, f32[4,1024]{1,0:T(4,128)S(1)} %get-tuple-element.369, ...), kind=kOutput, calls=%fused_computation.8.clone.1 | convolution fusion | flops 273678336 | bytes 8487936 | tf_op jit(solution)/shard_map/while/body/eval_jaxpr/grqk,kgd->grqd/dot_general | solution.py:38
  104.8 0.9 fusion.86
  105.7 1.6 bitcast_reduce_fusion.6
  107.3 2.7 %bitcast_add_fusion.13 = f32[1,4,1024,128]{3,2,1,0:T(8,128)S(1)} fusion(f32[1,4,1024,128]{3,2,1,0:T(8,128)S(1)} %get-tuple-element.432, f32[256,1024,4]{1,0,2:T(8,128)S(1)} %get-tuple-element.368, f32[4,1024]{1,0:T(4,128)S(1)} %bitcast.256, pred[]{:T(512)} %get-tuple-element.442, f32[4,1024]{1,0:T(4,128)S(1)} %get-tuple-element.369, ...), kind=kOutput, calls=%fused_computation.8.clone.1 | convolution fusion | flops 273678336 | bytes 8487936 | tf_op jit(solution)/shard_map/while/body/eval_jaxpr/grqk,kgd->grqd/dot_general | solution.py:38
  110.0 0.9 fusion.86
  110.9 1.6 bitcast_reduce_fusion.6
  112.5 2.7 %bitcast_add_fusion.13 = f32[1,4,1024,128]{3,2,1,0:T(8,128)S(1)} fusion(f32[1,4,1024,128]{3,2,1,0:T(8,128)S(1)} %get-tuple-element.432, f32[256,1024,4]{1,0,2:T(8,128)S(1)} %get-tuple-element.368, f32[4,1024]{1,0:T(4,128)S(1)} %bitcast.256, pred[]{:T(512)} %get-tuple-element.442, f32[4,1024]{1,0:T(4,128)S(1)} %get-tuple-element.369, ...), kind=kOutput, calls=%fused_computation.8.clone.1 | convolution fusion | flops 273678336 | bytes 8487936 | tf_op jit(solution)/shard_map/while/body/eval_jaxpr/grqk,kgd->grqd/dot_general | solution.py:38
  115.2 0.9 fusion.86
  116.2 20.8 %while.44 = (s32[]{:T(128)}, f32[1,4,1024]{2,1,0:T(4,128)S(1)}, f32[1,4,1024]{2,1,0:T(4,128)S(1)}, f32[1,4,1024,128]{3,2,1,0:T(8,128)S(1)}, pred[]{:T(512)}, /*i...) while((s32[]{:T(128)}, f32[1,4,1024]{2,1,0:T(4,128)S(1)}, ...), condition=%wide.region_11.12_spmd, body=%wide.region_8.11_spmd.sunk | while | flops 549466112 | bytes 18221148 | solution.py:47
  116.2 1.6 bitcast_reduce_fusion.7
  117.8 2.7 %bitcast_add_fusion.15 = f32[1,4,1024,128]{3,2,1,0:T(8,128)S(1)} fusion(f32[1,4,1024,128]{3,2,1,0:T(8,128)S(1)} %get-tuple-element.459, f32[256,1024,4]{1,0,2:T(8,128)S(1)} %get-tuple-element.380, f32[4,1024]{1,0:T(4,128)S(1)} %bitcast.258, pred[]{:T(512)} %get-tuple-element.469, f32[4,1024]{1,0:T(4,128)S(1)} %get-tuple-element.381, ...), kind=kOutput, calls=%fused_computation.35.clone.1 | convolution fusion | flops 273678336 | bytes 8487936 | tf_op jit(solution)/shard_map/while/body/eval_jaxpr/grqk,kgd->grqd/dot_general | solution.py:38
  120.4 0.9 fusion.90
  121.4 1.6 bitcast_reduce_fusion.7
  123.0 2.7 %bitcast_add_fusion.15 = f32[1,4,1024,128]{3,2,1,0:T(8,128)S(1)} fusion(f32[1,4,1024,128]{3,2,1,0:T(8,128)S(1)} %get-tuple-element.459, f32[256,1024,4]{1,0,2:T(8,128)S(1)} %get-tuple-element.380, f32[4,1024]{1,0:T(4,128)S(1)} %bitcast.258, pred[]{:T(512)} %get-tuple-element.469, f32[4,1024]{1,0:T(4,128)S(1)} %get-tuple-element.381, ...), kind=kOutput, calls=%fused_computation.35.clone.1 | convolution fusion | flops 273678336 | bytes 8487936 | tf_op jit(solution)/shard_map/while/body/eval_jaxpr/grqk,kgd->grqd/dot_general | solution.py:38
  125.7 0.9 fusion.90
  126.6 1.6 bitcast_reduce_fusion.7
  128.2 2.7 %bitcast_add_fusion.15 = f32[1,4,1024,128]{3,2,1,0:T(8,128)S(1)} fusion(f32[1,4,1024,128]{3,2,1,0:T(8,128)S(1)} %get-tuple-element.459, f32[256,1024,4]{1,0,2:T(8,128)S(1)} %get-tuple-element.380, f32[4,1024]{1,0:T(4,128)S(1)} %bitcast.258, pred[]{:T(512)} %get-tuple-element.469, f32[4,1024]{1,0:T(4,128)S(1)} %get-tuple-element.381, ...), kind=kOutput, calls=%fused_computation.35.clone.1 | convolution fusion | flops 273678336 | bytes 8487936 | tf_op jit(solution)/shard_map/while/body/eval_jaxpr/grqk,kgd->grqd/dot_general | solution.py:38
  130.9 0.9 fusion.90
  131.8 1.6 bitcast_reduce_fusion.7
  133.4 2.7 %bitcast_add_fusion.15 = f32[1,4,1024,128]{3,2,1,0:T(8,128)S(1)} fusion(f32[1,4,1024,128]{3,2,1,0:T(8,128)S(1)} %get-tuple-element.459, f32[256,1024,4]{1,0,2:T(8,128)S(1)} %get-tuple-element.380, f32[4,1024]{1,0:T(4,128)S(1)} %bitcast.258, pred[]{:T(512)} %get-tuple-element.469, f32[4,1024]{1,0:T(4,128)S(1)} %get-tuple-element.381, ...), kind=kOutput, calls=%fused_computation.35.clone.1 | convolution fusion | flops 273678336 | bytes 8487936 | tf_op jit(solution)/shard_map/while/body/eval_jaxpr/grqk,kgd->grqd/dot_general | solution.py:38
  136.1 0.9 fusion.90
  137.0 0.7 fusion.67
  137.7 0.9 fusion.66
  138.7 1.0 collective-permute-start.4
  140.1 2.7 %collective-permute-start.7 = (bf16[128,4,128]{2,0,1:T(8,128)(2,1)S(1)}, bf16[128,4,128]{2,0,1:T(8,128)(2,1)S(1)}, u32[]{:S(2)}, u32[]{:S(2)}) collective-permute-start(bf16[128,4,128]{2,0,1:T(8,128)(2,1)S(1)} %get-tuple-element.224), channel_id=1, source_target_pairs={{0,4},{1,5},{2,6},{3,7},{4,0},{5,1},{6,2},{7,3},{8,12},{9,13},{10,... | collective-permute-start | bytes 393224 | tf_op jit(solution)/shard_map/ppermute | solution.py:70
  142.9 0.8 collective-permute-done.4
  143.7 4.4 %collective-permute-done.5 = bf16[128,4,128]{2,0,1:T(8,128)(2,1)S(1)} collective-permute-done((bf16[128,4,128]{2,0,1:T(8,128)(2,1)S(1)}, bf16[128,4,128]{2,0,1:T(8,128)(2,1)S(1)}, u32[]{:S(2)}, u32[]{:S(2)}) %collective-permute-start.5) | collective-permute-done | bytes 131104 | tf_op jit(solution)/shard_map/ppermute | solution.py:70
  148.1 1.2 collective-permute-done.6
  149.3 12.1 %collective-permute-done.7 = bf16[128,4,128]{2,0,1:T(8,128)(2,1)S(1)} collective-permute-done((bf16[128,4,128]{2,0,1:T(8,128)(2,1)S(1)}, bf16[128,4,128]{2,0,1:T(8,128)(2,1)S(1)}, u32[]{:S(2)}, u32[]{:S(2)}) %collective-permute-start.7) | collective-permute-done | bytes 131104 | tf_op jit(solution)/shard_map/ppermute | solution.py:70
  161.4 1.2 collective-permute-done.8
  163.0 1.1 copy_bitcast_fusion
  (84 shorter events, 3.5 us)
Async XLA Ops:
  0.0 1.0 copy-start
  1.0 20.2 %copy-start.5 = (bf16[128,4096]{1,0:T(8,128)(2,1)S(1)}, bf16[128,4096]{1,0:T(8,128)(2,1)}, u32[]{:S(2)}) copy-start(bf16[128,4096]{1,0:T(8,128)(2,1)} %param.9) | copy-start | bytes 3145732
  1.7 16.1 %all-to-all-start = ((bf16[128,8,128]{2,0,1:T(8,128)(2,1)}), bf16[128,8,128]{2,0,1:T(8,128)(2,1)S(1)}, u32[]{:S(2)}, u32[]{:S(2)}) async-start(bf16[128,8,128]{2,0,1:T(8,128)(2,1)} %copy_bitcast_fusion.2), calls=%async_computation | async-start | bytes 524288 | tf_op jit(solution)/shard_map/all_to_all | solution.py:90
  17.8 13.1 %copy-start.3 = (bf16[128,8,128]{2,0,1:T(8,128)(2,1)}, bf16[128,8,128]{2,0,1:T(8,128)(2,1)S(1)}, u32[]{:S(2)}) copy-start(bf16[128,8,128]{2,0,1:T(8,128)(2,1)S(1)} %all-to-all-done) | copy-start | bytes 786436
  17.8 13.1 %all-to-all-start.2 = ((bf16[128,8,128]{2,0,1:T(8,128)(2,1)}), bf16[128,8,128]{2,0,1:T(8,128)(2,1)S(1)}, u32[]{:S(2)}, u32[]{:S(2)}) async-start(bf16[128,8,128]{2,0,1:T(8,128)(2,1)} %copy_bitcast_fusion.1), calls=%async_computation.2 | async-start | bytes 524288 | tf_op jit(solution)/shard_map/all_to_all | solution.py:91
  30.8 0.7 copy-start.4
  31.5 30.1 %all-to-all-start.1 = ((bf16[128,32,128]{0,2,1:T(8,128)(2,1)}), bf16[128,32,128]{0,2,1:T(8,128)(2,1)S(1)}, u32[]{:S(2)}, u32[]{:S(2)}) async-start(bf16[128,32,128]{0,2,1:T(8,128)(2,1)} %bitcast.31), calls=%async_computation.1 | async-start | bytes 2097152 | tf_op jit(solution)/shard_map/all_to_all | solution.py:89
  35.2 60.1 %collective-permute-start = (bf16[1024,1,128]{2,0,1:T(8,128)(2,1)}, bf16[1024,1,128]{2,0,1:T(8,128)(2,1)}, u32[]{:S(2)}, u32[]{:S(2)}) collective-permute-start(bf16[1024,1,128]{2,0,1:T(8,128)(2,1)} %bitcast.262), channel_id=1, source_target_pairs={{0,8},{8,16},{16,24},{1,9},{9,17},{17,25},{2,10},{10,18},{18,26},{... | collective-permute-start | bytes 786440 | tf_op jit(solution)/shard_map/ppermute | solution.py:14
  39.3 76.8 %collective-permute-start.2 = (bf16[1024,1,128]{2,0,1:T(8,128)(2,1)}, bf16[1024,1,128]{2,0,1:T(8,128)(2,1)}, u32[]{:S(2)}, u32[]{:S(2)}) collective-permute-start(bf16[1024,1,128]{2,0,1:T(8,128)(2,1)} %bitcast.263), channel_id=1, source_target_pairs={{8,0},{16,8},{24,16},{9,1},{17,9},{25,17},{10,2},{18,10},{26,18},{... | collective-permute-start | bytes 786440 | tf_op jit(solution)/shard_map/ppermute | solution.py:14
  40.6 54.7 %collective-permute-start.1 = (bf16[1024,1,128]{2,0,1:T(8,128)(2,1)}, bf16[1024,1,128]{2,0,1:T(8,128)(2,1)}, u32[]{:S(2)}, u32[]{:S(2)}) collective-permute-start(bf16[1024,1,128]{2,0,1:T(8,128)(2,1)} %bitcast.265), channel_id=1, source_target_pairs={{0,8},{8,16},{16,24},{1,9},{9,17},{17,25},{2,10},{10,18},{18,26},{... | collective-permute-start | bytes 786440 | tf_op jit(solution)/shard_map/ppermute | solution.py:14
  45.8 70.3 %collective-permute-start.3 = (bf16[1024,1,128]{2,0,1:T(8,128)(2,1)}, bf16[1024,1,128]{2,0,1:T(8,128)(2,1)}, u32[]{:S(2)}, u32[]{:S(2)}) collective-permute-start(bf16[1024,1,128]{2,0,1:T(8,128)(2,1)} %bitcast.266), channel_id=1, source_target_pairs={{8,0},{16,8},{24,16},{9,1},{17,9},{25,17},{10,2},{18,10},{26,18},{... | collective-permute-start | bytes 786440 | tf_op jit(solution)/shard_map/ppermute | solution.py:14
  61.6 1.0 copy-start.2
  67.7 3.5 %copy-start.1 = (f32[256,1024,4]{1,0,2:T(8,128)S(1)}, f32[256,1024,4]{1,0,2:T(8,128)}, u32[]{:S(2)}) copy-start(f32[256,1024,4]{1,0,2:T(8,128)} %get-tuple-element.391) | copy-start | bytes 12582916 | tf_op jit(solution)/shard_map/while
  75.5 3.5 %copy-start.1 = (f32[256,1024,4]{1,0,2:T(8,128)S(1)}, f32[256,1024,4]{1,0,2:T(8,128)}, u32[]{:S(2)}) copy-start(f32[256,1024,4]{1,0,2:T(8,128)} %get-tuple-element.391) | copy-start | bytes 12582916 | tf_op jit(solution)/shard_map/while
  83.3 3.5 %copy-start.1 = (f32[256,1024,4]{1,0,2:T(8,128)S(1)}, f32[256,1024,4]{1,0,2:T(8,128)}, u32[]{:S(2)}) copy-start(f32[256,1024,4]{1,0,2:T(8,128)} %get-tuple-element.391) | copy-start | bytes 12582916 | tf_op jit(solution)/shard_map/while
  91.1 3.5 %copy-start.1 = (f32[256,1024,4]{1,0,2:T(8,128)S(1)}, f32[256,1024,4]{1,0,2:T(8,128)}, u32[]{:S(2)}) copy-start(f32[256,1024,4]{1,0,2:T(8,128)} %get-tuple-element.391) | copy-start | bytes 12582916 | tf_op jit(solution)/shard_map/while
  138.7 4.9 %collective-permute-start.4 = (bf16[128,4,128]{2,0,1:T(8,128)(2,1)S(1)}, bf16[128,4,128]{2,0,1:T(8,128)(2,1)S(1)}, u32[]{:S(2)}, u32[]{:S(2)}) collective-permute-start(bf16[128,4,128]{2,0,1:T(8,128)(2,1)S(1)} %get-tuple-element.227), channel_id=1, source_target_pairs={{0,7},{1,0},{2,1},{3,2},{4,3},{5,4},{6,5},{7,6},{8,15},{9,8},{10,9... | collective-permute-start | bytes 393224 | tf_op jit(solution)/shard_map/ppermute | solution.py:70
  139.7 8.4 %collective-permute-start.5 = (bf16[128,4,128]{2,0,1:T(8,128)(2,1)S(1)}, bf16[128,4,128]{2,0,1:T(8,128)(2,1)S(1)}, u32[]{:S(2)}, u32[]{:S(2)}) collective-permute-start(bf16[128,4,128]{2,0,1:T(8,128)(2,1)S(1)} %get-tuple-element.226), channel_id=1, source_target_pairs={{0,6},{1,7},{2,0},{3,1},{4,2},{5,3},{6,4},{7,5},{8,14},{9,15},{10,... | collective-permute-start | bytes 393224 | tf_op jit(solution)/shard_map/ppermute | solution.py:70
  140.1 9.2 %collective-permute-start.6 = (bf16[128,4,128]{2,0,1:T(8,128)(2,1)S(1)}, bf16[128,4,128]{2,0,1:T(8,128)(2,1)S(1)}, u32[]{:S(2)}, u32[]{:S(2)}) collective-permute-start(bf16[128,4,128]{2,0,1:T(8,128)(2,1)S(1)} %get-tuple-element.225), channel_id=1, source_target_pairs={{0,5},{1,6},{2,7},{3,0},{4,1},{5,2},{6,3},{7,4},{8,13},{9,14},{10,... | collective-permute-start | bytes 393224 | tf_op jit(solution)/shard_map/ppermute | solution.py:70
  140.1 21.3 %collective-permute-start.7 = (bf16[128,4,128]{2,0,1:T(8,128)(2,1)S(1)}, bf16[128,4,128]{2,0,1:T(8,128)(2,1)S(1)}, u32[]{:S(2)}, u32[]{:S(2)}) collective-permute-start(bf16[128,4,128]{2,0,1:T(8,128)(2,1)S(1)} %get-tuple-element.224), channel_id=1, source_target_pairs={{0,4},{1,5},{2,6},{3,7},{4,0},{5,1},{6,2},{7,3},{8,12},{9,13},{10,... | collective-permute-start | bytes 393224 | tf_op jit(solution)/shard_map/ppermute | solution.py:70
  142.8 19.8 %collective-permute-start.8 = (bf16[128,4,128]{2,0,1:T(8,128)(2,1)S(1)}, bf16[128,4,128]{2,0,1:T(8,128)(2,1)S(1)}, u32[]{:S(2)}, u32[]{:S(2)}) collective-permute-start(bf16[128,4,128]{2,0,1:T(8,128)(2,1)S(1)} %get-tuple-element.223), channel_id=1, source_target_pairs={{0,3},{1,4},{2,5},{3,6},{4,7},{5,0},{6,1},{7,2},{8,11},{9,12},{10,... | collective-permute-start | bytes 393224 | tf_op jit(solution)/shard_map/ppermute | solution.py:70
  143.6 19.0 %collective-permute-start.9 = (bf16[128,4,128]{2,0,1:T(8,128)(2,1)S(1)}, bf16[128,4,128]{2,0,1:T(8,128)(2,1)S(1)}, u32[]{:S(2)}, u32[]{:S(2)}) collective-permute-start(bf16[128,4,128]{2,0,1:T(8,128)(2,1)S(1)} %get-tuple-element.222), channel_id=1, source_target_pairs={{0,2},{1,3},{2,4},{3,5},{4,6},{5,7},{6,0},{7,1},{8,10},{9,11},{10,... | collective-permute-start | bytes 393224 | tf_op jit(solution)/shard_map/ppermute | solution.py:70
  148.1 14.6 %collective-permute-start.10 = (bf16[128,4,128]{2,0,1:T(8,128)(2,1)S(1)}, bf16[128,4,128]{2,0,1:T(8,128)(2,1)S(1)}, u32[]{:S(2)}, u32[]{:S(2)}) collective-permute-start(bf16[128,4,128]{2,0,1:T(8,128)(2,1)S(1)} %get-tuple-element.221), channel_id=1, source_target_pairs={{0,1},{1,2},{2,3},{3,4},{4,5},{5,6},{6,7},{7,0},{8,9},{9,10},{10,1... | collective-permute-start | bytes 393224 | tf_op jit(solution)/shard_map/ppermute | solution.py:70
